TPU v7x, 128 devices: a whole 4x4x4 slice. The times are simulated.
128 devices in a mesh: section: 8 (over y, core), fsdp: 16 (over x, z).
Axes of the slice: x: 4, y: 4, z: 4, core: 2. Of those that a mesh axis runs over, the one named last changes fastest.
Arguments:
- layer_input: bfloat16 [8, 8192, 2048], P('section', 'fsdp'), may hold values from -6 to 6
- resid_grad: bfloat16 [8, 8192, 2048], P('section', 'fsdp'), may hold values from -6 to 6
- qkv_grad: bfloat16 [8, 8192, 3072], P('section', 'fsdp'), may hold values from -6 to 6
- prev_input: bfloat16 [8, 8192, 2048], P('section', 'fsdp'), may hold values from -6 to 6
- prev_qkv_grad: bfloat16 [8, 8192, 3072], P('section', 'fsdp'), may hold values from -0.059814453 to 0.059814453
- qkv_weight: bfloat16 [8, 2048, 3072], P('section', 'fsdp'), may hold values from -0.125 to 0.125
- norm_gain: float32 [8, 2048], P('section'), may hold values from 0.1 to 1.9
Outputs:
- upstream_grad: bfloat16 [8, 8192, 2048], P('section', 'fsdp')
- weight_grad: float32 [8, 2048, 3072], P('section', 'fsdp')
- gain_grad: float32 [8, 2048], P('section')
All inputs are finite; a program needn't handle non-finite values.
Results may differ from a plain program's by a relative error of at most 0.018.
Values may be sent and summed in bfloat16 or wider, within the bound.
A program may use at most 128 MiB of HBM per device.

v0:
```python
import jax
import jax.numpy as jnp
from jax import lax
from jax.sharding import PartitionSpec as P

EPS = 1e-05


def from_behind(block, axis, distance):
    devices = range(lax.axis_size(axis))
    route = [(i - distance, i) for i in devices if i - distance in devices]
    return lax.ppermute(block, axis, route)


def row_scale(rows):
    values = rows.astype(jnp.float32)
    return lax.rsqrt(jnp.mean(values * values, axis=-1, keepdims=True) + EPS)


def transpose_product(grads, piece):
    return lax.dot_general(
        grads, piece, (((1,), (1,)), ((), ())), preferred_element_type=jnp.float32
    )


def local(layer_input, resid_grad, qkv_grad, prev_input, prev_qkv_grad, qkv_weight, norm_gain):
    rows_now = layer_input[0]
    grads_now = qkv_grad[0]
    rows_prev = prev_input[0]
    grads_prev = prev_qkv_grad[0]
    weight_rows = qkv_weight[0]
    gain = norm_gain[0]
    owned = weight_rows.shape[0]
    prev_scale = row_scale(rows_prev)
    prev_normed = (rows_prev.astype(jnp.float32) * prev_scale * gain[None, :]).astype(jnp.bfloat16)
    direction = transpose_product(
        grads_now, lax.all_gather(weight_rows, "fsdp", axis=0, tiled=True)
    )
    scale = row_scale(rows_now)
    values = rows_now.astype(jnp.float32)
    gained = gain[None, :] * direction
    inner = jnp.mean(gained * values, axis=-1, keepdims=True)
    local_grad = (
        resid_grad[0].astype(jnp.float32) + scale * gained - values * scale * scale * scale * inner
    ).astype(jnp.bfloat16)
    upstream_grad = from_behind(local_grad, "section", -1)
    weight_grad = lax.psum_scatter(
        lax.dot_general(
            prev_normed, grads_prev, (((0,), (0,)), ((), ())), preferred_element_type=jnp.float32
        ).astype(jnp.bfloat16),
        "fsdp",
        scatter_dimension=0,
        tiled=True,
    ).astype(jnp.float32)
    owned_gain = lax.dynamic_slice_in_dim(gain, lax.axis_index("fsdp") * owned, owned, 0)
    gain_part = jnp.sum(weight_rows.astype(jnp.float32) * weight_grad, axis=1) / owned_gain
    gain_grad = lax.all_gather(gain_part, "fsdp", axis=0, tiled=True)
    return (upstream_grad[None], weight_grad[None], gain_grad[None])


def solution(mesh):
    placed = (
        P("section", "fsdp", None),
        P("section", "fsdp", None),
        P("section", "fsdp", None),
        P("section", "fsdp", None),
        P("section", "fsdp", None),
        P("section", "fsdp", None),
        P("section", None),
    )
    return jax.shard_map(
        local,
        mesh=mesh,
        in_specs=placed,
        out_specs=(P("section", "fsdp", None), P("section", "fsdp", None), P("section", None)),
        check_vma=False,
    )
```

profile of v0, /device:TPU:0, one launch (start us, length us, event | category | flops | bytes accessed | tf_op | source)
XLA Modules:
  0.0 234.6 jit_solution(13687583729323604503)
XLA Ops:
  7.2 0.0 copy-start
  7.2 0.0 all-gather.4.cloned.1.call-start
  7.2 0.7 all-gather.4.cloned.1.call-update
  7.9 0.0 reduce-scatter.2.cloned.1.call-start
  8.0 2.2 fusion.2
  10.2 0.0 copy-done
  10.2 11.6 %convolution_convert_fusion = bf16[2048,3072]{1,0:T(8,128)(2,1)} fusion(bf16[1,512,3072]{2,1,0:T(8,128)(2,1)S(1)} %copy-done, bf16[1,512,2048]{2,1,0:T(8,128)(2,1)} %param.10, f32[2048]{0:T(1024)} %bitcast.39, f32[512]{0:T(512)S(1)} %add_rsqrt_fusion), kind=kOutput, calls=%fused_computation.2 | convolution fusion | flops 6452936704 | bytes 17836032 | tf_op jit(solution)/shard_map/dot_general | solution.py:48
  21.8 0.0 copy-start.3
  21.8 0.0 reduce-scatter.2.cloned.1.call-update
  21.8 81.0 %all-gather.4.cloned.1.call-done = bf16[1,2048,3072]{2,1,0:T(8,128)(2,1)} async-done(((bf16[1,128,3072]{2,1,0:T(8,128)(2,1)}), bf16[1,2048,3072]{2,1,0:T(8,128)(2,1)}) %all-gather.4.cloned.1.call-update) | async-done | bytes 12582928 | tf_op jit(solution)/shard_map/all_gather | solution.py:37
  102.8 0.0 copy-done.3
  102.8 0.0 copy-start.1
  102.8 0.0 copy-start.2
  102.9 11.3 %fusion.5 = (f32[512]{0:T(512)S(1)}, f32[512]{0:T(512)S(1)}, f32[512,2048]{1,0:T(8,128)S(1)}) fusion(bf16[1,512,2048]{2,1,0:T(8,128)(2,1)} %param.7, f32[2048]{0:T(1024)S(1)} %bitcast.40, bf16[1,2048,3072]{2,1,0:T(8,128)(2,1)} %all-gather.4.cloned.1.call-done, bf16[1,512,3072]{2,1,0:T(8,128)(2,1)} %param.9), kind=kOutput, calls=%fused_computation.11 | convolution fusion | flops 6448741376 | bytes 22032384 | tf_op jit(solution)/shard_map/dot_general | solution.py:21
  114.2 0.0 copy-done.1
  114.2 0.0 copy-done.2
  114.2 3.1 %fusion.10 = bf16[512,2048]{1,0:T(8,128)(2,1)} fusion(f32[512,2048]{1,0:T(8,128)S(1)} %get-tuple-element.5, bf16[1,512,2048]{2,1,0:T(8,128)(2,1)S(1)} %copy-done.2, bf16[1,512,2048]{2,1,0:T(8,128)(2,1)S(1)} %copy-done.1, f32[512]{0:T(512)S(1)} %get-tuple-element.7, f32[2048]{0:T(1024)S(1)} %bitcast.41, f32[512]{0:T(512)S(1)} %get-tuple-element.6), kind=kLoop, calls=%fused_computation.16 | loop fusion | flops 11534336 | bytes 10498048 | tf_op jit(solution)/shard_map/convert_element_type | solution.py:45
  117.3 1.3 collective-permute-start
  118.6 82.1 %reduce-scatter.2.cloned.1.call-done = bf16[128,3072]{1,0:T(8,128)(2,1)} async-done(((bf16[2048,3072]{1,0:T(8,128)(2,1)}), bf16[128,3072]{1,0:T(8,128)(2,1)}) %reduce-scatter.2.cloned.1.call-update) | async-done | bytes 786448 | tf_op jit(solution)/shard_map/reduce_scatter | solution.py:47
  200.6 1.7 fusion.18
  202.3 19.3 %all-gather.1 = f32[16,1,128]{2,1,0:T(1,128)S(1)} all-gather(f32[1,1,128]{2,1,0:T(1,128)S(1)} %fusion.19), channel_id=1, replica_groups=mesh['section'=8,'fsdp'=16] {'fsdp'}, dimensions={0}, use_global_device_ids=true | all-gather | bytes 8704 | tf_op jit(solution)/shard_map/all_gather | solution.py:57
  221.6 2.4 %convert_bitcast_fusion = f32[1,128,3072]{2,1,0:T(8,128)} fusion(bf16[128,3072]{1,0:T(8,128)(2,1)} %reduce-scatter.2.cloned.1.call-done), kind=kLoop, calls=%fused_computation.25 | loop fusion | flops 393216 | bytes 2359296 | tf_op jit(solution)/shard_map/broadcast_in_dim | solution.py:58
  224.0 0.0 collective-permute-done
  224.0 3.2 %copy.12 = bf16[1,512,2048]{2,1,0:T(8,128)(2,1)} copy(bf16[1,512,2048]{2,1,0:T(8,128)(2,1)} %bitcast.6) | data formatting | bytes 4194304
  227.2 0.6 copy.13
  (3 shorter events, 0.0 us)
Async XLA Ops:
  7.2 3.0 %copy-start = (bf16[1,512,3072]{2,1,0:T(8,128)(2,1)S(1)}, bf16[1,512,3072]{2,1,0:T(8,128)(2,1)}, u32[]{:S(2)}) copy-start(bf16[1,512,3072]{2,1,0:T(8,128)(2,1)} %param.11) | copy-start | bytes 9437188
  7.2 95.7 %all-gather.4.cloned.1.call-start = ((), (), s32[]{:S(2)}) async-start(), calls=%async_computation.2 | async-start | bytes 13369344 | tf_op jit(solution)/shard_map/all_gather | solution.py:37
  7.9 192.7 %reduce-scatter.2.cloned.1.call-start = ((), (), s32[]{:S(2)}) async-start(), calls=%async_computation.1 | async-start | bytes 13369344 | tf_op jit(solution)/shard_map/reduce_scatter | solution.py:47
  21.8 81.1 %copy-start.3 = (f32[1,2048]{1,0:T(1,128)S(1)}, f32[1,2048]{1,0:T(1,128)}, u32[]{:S(2)}) copy-start(f32[1,2048]{1,0:T(1,128)} %param.13) | copy-start | bytes 24580
  102.8 11.3 %copy-start.1 = (bf16[1,512,2048]{2,1,0:T(8,128)(2,1)S(1)}, bf16[1,512,2048]{2,1,0:T(8,128)(2,1)}, u32[]{:S(2)}) copy-start(bf16[1,512,2048]{2,1,0:T(8,128)(2,1)} %param.7) | copy-start | bytes 6291460
  102.8 11.3 %copy-start.2 = (bf16[1,512,2048]{2,1,0:T(8,128)(2,1)S(1)}, bf16[1,512,2048]{2,1,0:T(8,128)(2,1)}, u32[]{:S(2)}) copy-start(bf16[1,512,2048]{2,1,0:T(8,128)(2,1)} %param.8) | copy-start | bytes 6291460
  117.3 106.7 %collective-permute-start = (bf16[512,2048]{1,0:T(8,128)(2,1)}, bf16[512,2048]{1,0:T(8,128)(2,1)}, u32[]{:S(2)}, u32[]{:S(2)}) collective-permute-start(bf16[512,2048]{1,0:T(8,128)(2,1)} %fusion.10), channel_id=1, source_target_pairs={{16,0},{32,16},{48,32},{64,48},{80,64},{96,80},{112,96},{17,1},{33... | collective-permute-start | bytes 6291464 | tf_op jit(solution)/shard_map/ppermute | solution.py:12
Sparse Core Ops, SparseCore 0:
  10.2 92.5 all-gather.3
  106.3 94.3 reduce-scatter.1
where the time goes:
time: 235 us
  waiting for transfers between devices  164 us (70%)
  matrix products  22.9 us (10%)
  blocking collectives  19.3 us (8%)
  between operations  14.1 us (6%)
  other arithmetic  9.45 us (4%)
  local copies, waits for them, and re-layouts  3.78 us (2%)
    reduce_scatter x1, waiting for transfers between devices, local(): lax.psum_scatter(lax.dot_general(prev_normed, grads_prev, (((0,), (0,)),...  82.1 us
    all_gather x1, waiting for transfers between devices, local(): lax.all_gather(weight_rows, 'fsdp', axis=0, tiled=True)  81 us
    all_gather x1, blocking collectives, local(): gain_grad = lax.all_gather(gain_part, 'fsdp', axis=0, tiled=True)  19.3 us
    dot_general x1, matrix products, local(): lax.dot_general(prev_normed, grads_prev, (((0,), (0,)), ((), ())), prefer...  11.6 us
    dot_general x1, matrix products, transpose_product(): lax.dot_general(grads, piece, (((1,), (1,)), ((), ())), preferred_element...  11.3 us
  transfers between devices with their start and end apart: 3, of which 2 were waited for; matrix products, arithmetic and copies ran while one was open for 14% of the time, Pallas kernels for 0%

commit v1 on v0

--- a/solution.py
+++ b/solution.py
@@ -4,6 +4,30 @@
 from jax.sharding import PartitionSpec as P
 
 EPS = 1e-05
+
+
+def handle_tasks_all(patch):
+    peer_axis = "fsdp"
+    carry_out = lax.axis_size(peer_axis)
+    near = lax.axis_index(peer_axis)
+    earlier, current_value, tile_out = (carry_out, near, patch.shape[0])
+    runs = [(to_i, (to_i + 1) % earlier) for to_i in range(earlier)]
+    history = [(to_i, (to_i - 1) % earlier) for to_i in range(earlier)]
+    wide_out = jnp.zeros((*patch.shape[:0], earlier * tile_out, *patch.shape[1:]), patch.dtype)
+    wide_out = lax.dynamic_update_slice_in_dim(wide_out, patch, current_value * tile_out, axis=0)
+    latest = top = patch
+    z1 = earlier // 2
+    for t in [*range(1, z1 + 1)]:
+        latest = lax.ppermute(latest, peer_axis, runs)
+        wide_out = lax.dynamic_update_slice_in_dim(
+            wide_out, latest, (current_value - t) % earlier * tile_out, axis=0
+        )
+        if t < earlier - z1:
+            top = lax.ppermute(top, peer_axis, perm=history)
+            wide_out = lax.dynamic_update_slice_in_dim(
+                wide_out, top, (current_value + t) % earlier * tile_out, axis=0
+            )
+    return wide_out
 
 
 def from_behind(block, axis, distance):
@@ -54,7 +78,7 @@
     ).astype(jnp.float32)
     owned_gain = lax.dynamic_slice_in_dim(gain, lax.axis_index("fsdp") * owned, owned, 0)
     gain_part = jnp.sum(weight_rows.astype(jnp.float32) * weight_grad, axis=1) / owned_gain
-    gain_grad = lax.all_gather(gain_part, "fsdp", axis=0, tiled=True)
+    gain_grad = handle_tasks_all(gain_part)
     return (upstream_grad[None], weight_grad[None], gain_grad[None])
 
 

time: 235 us -> 269 us (1.14)
  starting transfers between devices: 1.36 us -> 38.9 us
  blocking collectives: 19.3 us -> 0 us
  waiting for transfers between devices: 164 us -> 179 us
    ppermute x0 -> x15, starting transfers between devices: none -> 37.6 us  [the longest x7 36.5 us: handle_tasks_all(): top = lax.ppermute(top, peer_axis, perm=history)]
    all_gather x1 -> x0, blocking collectives: 19.3 us -> none  [local(): gain_grad = lax.all_gather(gain_part, 'fsdp', axis=0, tiled=True)]
    ppermute x0 -> x15, waiting for transfers between devices: none -> 15.8 us  [the longest x8 15.8 us: handle_tasks_all(): latest = lax.ppermute(latest, peer_axis, runs)]
  transfers between devices with their start and end apart: 3 -> 18, of which waited for: 2 -> 9; matrix products, arithmetic and copies ran while one was open for 14% -> 12% of each run, Pallas kernels for 0% -> 0%
where the time goes in v1:
time: 269 us; the launch traced here: 268 us
  waiting for transfers between devices  179 us (67%)
  starting transfers between devices  38.9 us (14%)
  matrix products  22.9 us (9%)
  between operations  14.4 us (5%)
  other arithmetic  9.46 us (4%)
  local copies, waits for them, and re-layouts  3.31 us (1%)
    reduce_scatter x1, waiting for transfers between devices, local(): lax.psum_scatter(lax.dot_general(prev_normed, grads_prev, (((0,), (0,)),...  82 us
    all_gather x1, waiting for transfers between devices, local(): lax.all_gather(weight_rows, 'fsdp', axis=0, tiled=True)  80.8 us
    ppermute x7, starting transfers between devices, handle_tasks_all(): top = lax.ppermute(top, peer_axis, perm=history)  36.5 us
    ppermute x8, waiting for transfers between devices, handle_tasks_all(): latest = lax.ppermute(latest, peer_axis, runs)  15.8 us
    dot_general x1, matrix products, local(): lax.dot_general(prev_normed, grads_prev, (((0,), (0,)), ((), ())), prefer...  11.6 us
    dot_general x1, matrix products, transpose_product(): lax.dot_general(grads, piece, (((1,), (1,)), ((), ())), preferred_element...  11.3 us
  transfers between devices with their start and end apart: 18, of which 9 were waited for; matrix products, arithmetic and copies ran while one was open for 12% of the time, Pallas kernels for 0%

profile of v1, /device:TPU:0, one launch (start us, length us, event | category | flops | bytes accessed | tf_op | source)
XLA Modules:
  0.0 268.3 jit_solution(15597129713506685397)
XLA Ops:
  7.2 0.0 copy-start
  7.2 0.0 all-gather.3.cloned.1.call-start
  7.2 0.7 all-gather.3.cloned.1.call-update
  7.9 0.0 reduce-scatter.2.cloned.1.call-start
  8.0 2.2 fusion.2
  10.2 0.0 copy-done
  10.2 11.6 %convolution_convert_fusion = bf16[2048,3072]{1,0:T(8,128)(2,1)} fusion(bf16[1,512,3072]{2,1,0:T(8,128)(2,1)S(1)} %copy-done, bf16[1,512,2048]{2,1,0:T(8,128)(2,1)} %param.10, f32[2048]{0:T(1024)} %bitcast.65, f32[512]{0:T(512)S(1)} %add_rsqrt_fusion), kind=kOutput, calls=%fused_computation.2 | convolution fusion | flops 6452936704 | bytes 17836032 | tf_op jit(solution)/shard_map/dot_general | solution.py:72
  21.8 0.0 copy-start.3
  21.8 0.0 reduce-scatter.2.cloned.1.call-update
  22.1 80.8 %all-gather.3.cloned.1.call-done = bf16[1,2048,3072]{2,1,0:T(8,128)(2,1)} async-done(((bf16[1,128,3072]{2,1,0:T(8,128)(2,1)}), bf16[1,2048,3072]{2,1,0:T(8,128)(2,1)}) %all-gather.3.cloned.1.call-update) | async-done | bytes 12582928 | tf_op jit(solution)/shard_map/all_gather | solution.py:61
  102.8 0.0 copy-done.3
  102.8 0.0 copy-start.1
  102.8 0.0 copy-start.2
  102.9 11.3 %fusion.5 = (f32[512]{0:T(512)S(1)}, f32[512]{0:T(512)S(1)}, f32[512,2048]{1,0:T(8,128)S(1)}) fusion(bf16[1,512,2048]{2,1,0:T(8,128)(2,1)} %param.7, f32[2048]{0:T(1024)S(1)} %bitcast.66, bf16[1,2048,3072]{2,1,0:T(8,128)(2,1)} %all-gather.3.cloned.1.call-done, bf16[1,512,3072]{2,1,0:T(8,128)(2,1)} %param.9), kind=kOutput, calls=%fused_computation.11 | convolution fusion | flops 6448741376 | bytes 22032384 | tf_op jit(solution)/shard_map/dot_general | solution.py:45
  114.2 0.0 copy-done.1
  114.2 0.0 copy-done.2
  114.2 3.1 %fusion.10 = bf16[512,2048]{1,0:T(8,128)(2,1)} fusion(f32[512,2048]{1,0:T(8,128)S(1)} %get-tuple-element.5, bf16[1,512,2048]{2,1,0:T(8,128)(2,1)S(1)} %copy-done.2, bf16[1,512,2048]{2,1,0:T(8,128)(2,1)S(1)} %copy-done.1, f32[512]{0:T(512)S(1)} %get-tuple-element.7, f32[2048]{0:T(1024)S(1)} %bitcast.67, f32[512]{0:T(512)S(1)} %get-tuple-element.6), kind=kLoop, calls=%fused_computation.16 | loop fusion | flops 11534336 | bytes 10498048 | tf_op jit(solution)/shard_map/convert_element_type | solution.py:69
  117.3 1.3 collective-permute-start
  118.6 82.0 %reduce-scatter.2.cloned.1.call-done = bf16[128,3072]{1,0:T(8,128)(2,1)} async-done(((bf16[2048,3072]{1,0:T(8,128)(2,1)}), bf16[128,3072]{1,0:T(8,128)(2,1)}) %reduce-scatter.2.cloned.1.call-update) | async-done | bytes 786448 | tf_op jit(solution)/shard_map/reduce_scatter | solution.py:71
  200.6 1.7 fusion.18
  202.3 0.9 collective-permute-start.1
  203.2 4.5 %collective-permute-start.2 = (f32[128]{0:T(128)S(1)}, f32[128]{0:T(128)S(1)}, u32[]{:S(2)}, u32[]{:S(2)}) collective-permute-start(f32[128]{0:T(128)S(1)} %bitcast_divide_fusion), channel_id=1, source_target_pairs={{0,15},{1,0},{2,1},{3,2},{4,3},{5,4},{6,5},{7,6},{8,7},{9,8},{10,9... | collective-permute-start | bytes 1544 | tf_op jit(solution)/shard_map/ppermute | solution.py:26
  207.7 2.4 convert_bitcast_fusion
  210.1 0.0 collective-permute-done.1
  210.2 0.1 collective-permute-start.3
  210.2 0.0 collective-permute-done.2
  210.3 5.3 %collective-permute-start.4 = (f32[128]{0:T(128)S(1)}, f32[128]{0:T(128)S(1)}, u32[]{:S(2)}, u32[]{:S(2)}) collective-permute-start(f32[128]{0:T(128)S(1)} %collective-permute-done.2), channel_id=1, source_target_pairs={{0,15},{1,0},{2,1},{3,2},{4,3},{5,4},{6,5},{7,6},{8,7},{9,8},{10,9... | collective-permute-start | bytes 1544 | tf_op jit(solution)/shard_map/ppermute | solution.py:26
  215.6 1.5 collective-permute-done.3
  217.1 0.0 collective-permute-start.5
  217.1 0.0 collective-permute-done.4
  217.1 5.3 %collective-permute-start.6 = (f32[128]{0:T(128)S(1)}, f32[128]{0:T(128)S(1)}, u32[]{:S(2)}, u32[]{:S(2)}) collective-permute-start(f32[128]{0:T(128)S(1)} %collective-permute-done.4), channel_id=1, source_target_pairs={{0,15},{1,0},{2,1},{3,2},{4,3},{5,4},{6,5},{7,6},{8,7},{9,8},{10,9... | collective-permute-start | bytes 1544 | tf_op jit(solution)/shard_map/ppermute | solution.py:26
  222.5 1.5 collective-permute-done.5
  223.9 0.0 collective-permute-start.7
  224.0 0.0 collective-permute-done.6
  224.0 5.3 %collective-permute-start.8 = (f32[128]{0:T(128)S(1)}, f32[128]{0:T(128)S(1)}, u32[]{:S(2)}, u32[]{:S(2)}) collective-permute-start(f32[128]{0:T(128)S(1)} %collective-permute-done.6), channel_id=1, source_target_pairs={{0,15},{1,0},{2,1},{3,2},{4,3},{5,4},{6,5},{7,6},{8,7},{9,8},{10,9... | collective-permute-start | bytes 1544 | tf_op jit(solution)/shard_map/ppermute | solution.py:26
  229.3 1.5 collective-permute-done.7
  230.8 0.0 collective-permute-start.9
  230.8 0.0 collective-permute-done.8
  230.8 5.3 %collective-permute-start.10 = (f32[128]{0:T(128)S(1)}, f32[128]{0:T(128)S(1)}, u32[]{:S(2)}, u32[]{:S(2)}) collective-permute-start(f32[128]{0:T(128)S(1)} %collective-permute-done.8), channel_id=1, source_target_pairs={{0,15},{1,0},{2,1},{3,2},{4,3},{5,4},{6,5},{7,6},{8,7},{9,8},{10,9... | collective-permute-start | bytes 1544 | tf_op jit(solution)/shard_map/ppermute | solution.py:26
  236.2 1.5 collective-permute-done.9
  237.7 0.0 collective-permute-start.11
  237.7 0.0 collective-permute-done.10
  237.7 5.3 %collective-permute-start.12 = (f32[128]{0:T(128)S(1)}, f32[128]{0:T(128)S(1)}, u32[]{:S(2)}, u32[]{:S(2)}) collective-permute-start(f32[128]{0:T(128)S(1)} %collective-permute-done.10), channel_id=1, source_target_pairs={{0,15},{1,0},{2,1},{3,2},{4,3},{5,4},{6,5},{7,6},{8,7},{9,8},{10,9... | collective-permute-start | bytes 1544 | tf_op jit(solution)/shard_map/ppermute | solution.py:26
  243.0 1.5 collective-permute-done.11
  244.5 0.0 collective-permute-start.13
  244.5 0.0 collective-permute-done.12
  244.5 5.3 %collective-permute-start.14 = (f32[128]{0:T(128)S(1)}, f32[128]{0:T(128)S(1)}, u32[]{:S(2)}, u32[]{:S(2)}) collective-permute-start(f32[128]{0:T(128)S(1)} %collective-permute-done.12), channel_id=1, source_target_pairs={{0,15},{1,0},{2,1},{3,2},{4,3},{5,4},{6,5},{7,6},{8,7},{9,8},{10,9... | collective-permute-start | bytes 1544 | tf_op jit(solution)/shard_map/ppermute | solution.py:26
  249.9 1.5 collective-permute-done.13
  251.4 0.0 collective-permute-start.15
  251.4 0.0 collective-permute-done.14
  251.4 6.8 %collective-permute-done.15 = f32[128]{0:T(128)S(1)} collective-permute-done((f32[128]{0:T(128)S(1)}, f32[128]{0:T(128)S(1)}, u32[]{:S(2)}, u32[]{:S(2)}) %collective-permute-start.15) | collective-permute-done | bytes 544 | tf_op jit(solution)/shard_map/ppermute | solution.py:21
  258.3 0.0 copy-start.4
  258.3 0.0 collective-permute-done
  258.3 3.2 %copy.27 = bf16[1,512,2048]{2,1,0:T(8,128)(2,1)} copy(bf16[1,512,2048]{2,1,0:T(8,128)(2,1)} %bitcast.6) | data formatting | bytes 4194304
  261.4 0.0 copy-done.4
  (20 shorter events, 0.2 us)
Async XLA Ops:
  7.2 3.0 %copy-start = (bf16[1,512,3072]{2,1,0:T(8,128)(2,1)S(1)}, bf16[1,512,3072]{2,1,0:T(8,128)(2,1)}, u32[]{:S(2)}) copy-start(bf16[1,512,3072]{2,1,0:T(8,128)(2,1)} %param.11) | copy-start | bytes 9437188
  7.2 95.7 %all-gather.3.cloned.1.call-start = ((), (), s32[]{:S(2)}) async-start(), calls=%async_computation.2 | async-start | bytes 13369344 | tf_op jit(solution)/shard_map/all_gather | solution.py:61
  7.9 192.7 %reduce-scatter.2.cloned.1.call-start = ((), (), s32[]{:S(2)}) async-start(), calls=%async_computation.1 | async-start | bytes 13369344 | tf_op jit(solution)/shard_map/reduce_scatter | solution.py:71
  21.8 81.1 %copy-start.3 = (f32[1,2048]{1,0:T(1,128)S(1)}, f32[1,2048]{1,0:T(1,128)}, u32[]{:S(2)}) copy-start(f32[1,2048]{1,0:T(1,128)} %param.13) | copy-start | bytes 24580
  102.8 11.3 %copy-start.1 = (bf16[1,512,2048]{2,1,0:T(8,128)(2,1)S(1)}, bf16[1,512,2048]{2,1,0:T(8,128)(2,1)}, u32[]{:S(2)}) copy-start(bf16[1,512,2048]{2,1,0:T(8,128)(2,1)} %param.7) | copy-start | bytes 6291460
  102.8 11.3 %copy-start.2 = (bf16[1,512,2048]{2,1,0:T(8,128)(2,1)S(1)}, bf16[1,512,2048]{2,1,0:T(8,128)(2,1)}, u32[]{:S(2)}) copy-start(bf16[1,512,2048]{2,1,0:T(8,128)(2,1)} %param.8) | copy-start | bytes 6291460
  117.3 141.0 %collective-permute-start = (bf16[512,2048]{1,0:T(8,128)(2,1)}, bf16[512,2048]{1,0:T(8,128)(2,1)}, u32[]{:S(2)}, u32[]{:S(2)}) collective-permute-start(bf16[512,2048]{1,0:T(8,128)(2,1)} %fusion.10), channel_id=1, source_target_pairs={{16,0},{32,16},{48,32},{64,48},{80,64},{96,80},{112,96},{17,1},{33... | collective-permute-start | bytes 6291464 | tf_op jit(solution)/shard_map/ppermute | solution.py:36
  202.3 7.9 %collective-permute-start.1 = (f32[128]{0:T(128)S(1)}, f32[128]{0:T(128)S(1)}, u32[]{:S(2)}, u32[]{:S(2)}) collective-permute-start(f32[128]{0:T(128)S(1)} %bitcast_divide_fusion), channel_id=1, source_target_pairs={{0,1},{1,2},{2,3},{3,4},{4,5},{5,6},{6,7},{7,8},{8,9},{9,10},{10,1... | collective-permute-start | bytes 1544 | tf_op jit(solution)/shard_map/ppermute | solution.py:21
  203.2 7.0 %collective-permute-start.2 = (f32[128]{0:T(128)S(1)}, f32[128]{0:T(128)S(1)}, u32[]{:S(2)}, u32[]{:S(2)}) collective-permute-start(f32[128]{0:T(128)S(1)} %bitcast_divide_fusion), channel_id=1, source_target_pairs={{0,15},{1,0},{2,1},{3,2},{4,3},{5,4},{6,5},{7,6},{8,7},{9,8},{10,9... | collective-permute-start | bytes 1544 | tf_op jit(solution)/shard_map/ppermute | solution.py:26
  210.2 6.9 %collective-permute-start.3 = (f32[128]{0:T(128)S(1)}, f32[128]{0:T(128)S(1)}, u32[]{:S(2)}, u32[]{:S(2)}) collective-permute-start(f32[128]{0:T(128)S(1)} %collective-permute-done.1), channel_id=1, source_target_pairs={{0,1},{1,2},{2,3},{3,4},{4,5},{5,6},{6,7},{7,8},{8,9},{9,10},{10,1... | collective-permute-start | bytes 1544 | tf_op jit(solution)/shard_map/ppermute | solution.py:21
  210.3 6.8 %collective-permute-start.4 = (f32[128]{0:T(128)S(1)}, f32[128]{0:T(128)S(1)}, u32[]{:S(2)}, u32[]{:S(2)}) collective-permute-start(f32[128]{0:T(128)S(1)} %collective-permute-done.2), channel_id=1, source_target_pairs={{0,15},{1,0},{2,1},{3,2},{4,3},{5,4},{6,5},{7,6},{8,7},{9,8},{10,9... | collective-permute-start | bytes 1544 | tf_op jit(solution)/shard_map/ppermute | solution.py:26
  217.1 6.9 %collective-permute-start.5 = (f32[128]{0:T(128)S(1)}, f32[128]{0:T(128)S(1)}, u32[]{:S(2)}, u32[]{:S(2)}) collective-permute-start(f32[128]{0:T(128)S(1)} %collective-permute-done.3), channel_id=1, source_target_pairs={{0,1},{1,2},{2,3},{3,4},{4,5},{5,6},{6,7},{7,8},{8,9},{9,10},{10,1... | collective-permute-start | bytes 1544 | tf_op jit(solution)/shard_map/ppermute | solution.py:21
  217.1 6.9 %collective-permute-start.6 = (f32[128]{0:T(128)S(1)}, f32[128]{0:T(128)S(1)}, u32[]{:S(2)}, u32[]{:S(2)}) collective-permute-start(f32[128]{0:T(128)S(1)} %collective-permute-done.4), channel_id=1, source_target_pairs={{0,15},{1,0},{2,1},{3,2},{4,3},{5,4},{6,5},{7,6},{8,7},{9,8},{10,9... | collective-permute-start | bytes 1544 | tf_op jit(solution)/shard_map/ppermute | solution.py:26
  223.9 6.9 %collective-permute-start.7 = (f32[128]{0:T(128)S(1)}, f32[128]{0:T(128)S(1)}, u32[]{:S(2)}, u32[]{:S(2)}) collective-permute-start(f32[128]{0:T(128)S(1)} %collective-permute-done.5), channel_id=1, source_target_pairs={{0,1},{1,2},{2,3},{3,4},{4,5},{5,6},{6,7},{7,8},{8,9},{9,10},{10,1... | collective-permute-start | bytes 1544 | tf_op jit(solution)/shard_map/ppermute | solution.py:21
  224.0 6.9 %collective-permute-start.8 = (f32[128]{0:T(128)S(1)}, f32[128]{0:T(128)S(1)}, u32[]{:S(2)}, u32[]{:S(2)}) collective-permute-start(f32[128]{0:T(128)S(1)} %collective-permute-done.6), channel_id=1, source_target_pairs={{0,15},{1,0},{2,1},{3,2},{4,3},{5,4},{6,5},{7,6},{8,7},{9,8},{10,9... | collective-permute-start | bytes 1544 | tf_op jit(solution)/shard_map/ppermute | solution.py:26
  230.8 6.9 %collective-permute-start.9 = (f32[128]{0:T(128)S(1)}, f32[128]{0:T(128)S(1)}, u32[]{:S(2)}, u32[]{:S(2)}) collective-permute-start(f32[128]{0:T(128)S(1)} %collective-permute-done.7), channel_id=1, source_target_pairs={{0,1},{1,2},{2,3},{3,4},{4,5},{5,6},{6,7},{7,8},{8,9},{9,10},{10,1... | collective-permute-start | bytes 1544 | tf_op jit(solution)/shard_map/ppermute | solution.py:21
  230.8 6.9 %collective-permute-start.10 = (f32[128]{0:T(128)S(1)}, f32[128]{0:T(128)S(1)}, u32[]{:S(2)}, u32[]{:S(2)}) collective-permute-start(f32[128]{0:T(128)S(1)} %collective-permute-done.8), channel_id=1, source_target_pairs={{0,15},{1,0},{2,1},{3,2},{4,3},{5,4},{6,5},{7,6},{8,7},{9,8},{10,9... | collective-permute-start | bytes 1544 | tf_op jit(solution)/shard_map/ppermute | solution.py:26
  237.7 6.9 %collective-permute-start.11 = (f32[128]{0:T(128)S(1)}, f32[128]{0:T(128)S(1)}, u32[]{:S(2)}, u32[]{:S(2)}) collective-permute-start(f32[128]{0:T(128)S(1)} %collective-permute-done.9), channel_id=1, source_target_pairs={{0,1},{1,2},{2,3},{3,4},{4,5},{5,6},{6,7},{7,8},{8,9},{9,10},{10,1... | collective-permute-start | bytes 1544 | tf_op jit(solution)/shard_map/ppermute | solution.py:21
  237.7 6.9 %collective-permute-start.12 = (f32[128]{0:T(128)S(1)}, f32[128]{0:T(128)S(1)}, u32[]{:S(2)}, u32[]{:S(2)}) collective-permute-start(f32[128]{0:T(128)S(1)} %collective-permute-done.10), channel_id=1, source_target_pairs={{0,15},{1,0},{2,1},{3,2},{4,3},{5,4},{6,5},{7,6},{8,7},{9,8},{10,9... | collective-permute-start | bytes 1544 | tf_op jit(solution)/shard_map/ppermute | solution.py:26
  244.5 6.9 %collective-permute-start.13 = (f32[128]{0:T(128)S(1)}, f32[128]{0:T(128)S(1)}, u32[]{:S(2)}, u32[]{:S(2)}) collective-permute-start(f32[128]{0:T(128)S(1)} %collective-permute-done.11), channel_id=1, source_target_pairs={{0,1},{1,2},{2,3},{3,4},{4,5},{5,6},{6,7},{7,8},{8,9},{9,10},{10,1... | collective-permute-start | bytes 1544 | tf_op jit(solution)/shard_map/ppermute | solution.py:21
  244.5 6.9 %collective-permute-start.14 = (f32[128]{0:T(128)S(1)}, f32[128]{0:T(128)S(1)}, u32[]{:S(2)}, u32[]{:S(2)}) collective-permute-start(f32[128]{0:T(128)S(1)} %collective-permute-done.12), channel_id=1, source_target_pairs={{0,15},{1,0},{2,1},{3,2},{4,3},{5,4},{6,5},{7,6},{8,7},{9,8},{10,9... | collective-permute-start | bytes 1544 | tf_op jit(solution)/shard_map/ppermute | solution.py:26
  251.4 6.9 %collective-permute-start.15 = (f32[128]{0:T(128)S(1)}, f32[128]{0:T(128)S(1)}, u32[]{:S(2)}, u32[]{:S(2)}) collective-permute-start(f32[128]{0:T(128)S(1)} %collective-permute-done.13), channel_id=1, source_target_pairs={{0,1},{1,2},{2,3},{3,4},{4,5},{5,6},{6,7},{7,8},{8,9},{9,10},{10,1... | collective-permute-start | bytes 1544 | tf_op jit(solution)/shard_map/ppermute | solution.py:21
  258.3 3.2 %copy-start.4 = (f32[1,2048]{1,0:T(1,128)}, f32[1,2048]{1,0:T(1,128)S(1)}, u32[]{:S(2)}) copy-start(f32[1,2048]{1,0:T(1,128)S(1)} %constant_dynamic-update-slice_fusion) | copy-start | bytes 24580
Sparse Core Ops, SparseCore 0:
  10.2 92.5 all-gather.2
  106.3 94.2 reduce-scatter.1
